TPU v7x, 32 devices: a whole 2x2x4 slice. The times are simulated.
32 devices in a mesh: pipe: 4 (over z), ctx: 4 (over y, x), exp: 2 (over core).
Axes of the slice: x: 2, y: 2, z: 4, core: 2. Of those that a mesh axis runs over, the one named last changes fastest.
Arguments:
- mix_input: bfloat16 [4, 512, 8192], P('pipe', 'ctx', 'exp'), may hold values from -6 to 6
- state_write: bfloat16 [4, 512, 64], P('pipe', 'ctx'), may hold values from -2.5 to 2.5
- state_read: bfloat16 [4, 512, 64], P('pipe', 'ctx'), may hold values from -2.5 to 2.5
- log_decay: float32 [4, 512, 128], P('pipe', 'ctx', 'exp'), may hold values from -1 to 0
- skip_gain: float32 [128], P('exp'), may hold values from 0.5 to 1.5
- query_rows: bfloat16 [4, 512, 8192], P('pipe', 'ctx', 'exp'), may hold values from -39.774756 to 39.774756
- key_rows: bfloat16 [4, 512, 1024], P('pipe', 'ctx', 'exp'), may hold values from -8 to 8
- value_rows: bfloat16 [4, 512, 1024], P('pipe', 'ctx', 'exp'), may hold values from -6 to 6
- incoming: bfloat16 [512, 8192], P('ctx', 'exp'), may hold values from -6 to 6
- norm_gain: float32 [8192], P('exp'), may hold values from 0.5 to 1.5
Outputs:
- mamba_out: bfloat16 [4, 512, 8192], P('pipe', 'ctx', 'exp')
- block_out: bfloat16 [4, 512, 8192], P('pipe', 'ctx', 'exp')
All inputs are finite; a program needn't handle non-finite values.
Results may differ from a plain program's by a relative error of at most 0.013.
Values may be sent and summed in bfloat16 or wider, within the bound.
A program may use at most 128 MiB of HBM per device.

v0:
```python
import math

import jax
import jax.numpy as jnp
from jax import lax
from jax.sharding import PartitionSpec as P

D = 8192
HEAD_DIM = 128


def entering_2(x, axis, join, neutral):
    place = lax.axis_index(axis)
    gathered = jax.tree.map(
        lambda a, kind: lax.all_gather(a.astype(kind), axis), x, (jnp.bfloat16, jnp.bfloat16)
    )
    state = jax.tree.map(lambda a, e: jnp.zeros_like(a) + jnp.asarray(e, a.dtype), x, neutral)

    def one(turn, state):
        return join(
            state,
            jax.tree.map(
                lambda a, own: lax.dynamic_index_in_dim(a, turn, 0, False).astype(own.dtype),
                gathered,
                x,
            ),
        )

    return lax.fori_loop(0, place, one, state)


def shifted(block, axis, distance):
    devices = range(lax.axis_size(axis))
    route = [(i - distance, i) for i in devices if i - distance in devices]
    return lax.ppermute(block, axis, route)


def merge_states(earlier, later):
    return (earlier[0] * later[0], later[0][:, None, None] * earlier[1] + later[1])


def split_halves(wide):
    upper_part = wide.astype(jnp.bfloat16)
    lower_part = (wide - upper_part.astype(jnp.float32)).astype(jnp.bfloat16)
    return (upper_part, lower_part)


def wide_first(form, wide, narrow):
    upper_part, lower_part = split_halves(wide)
    return jnp.einsum(form, upper_part, narrow, preferred_element_type=jnp.float32) + jnp.einsum(
        form, lower_part, narrow, preferred_element_type=jnp.float32
    )


def wide_second(form, narrow, wide):
    upper_part, lower_part = split_halves(wide)
    return jnp.einsum(form, narrow, upper_part, preferred_element_type=jnp.float32) + jnp.einsum(
        form, narrow, lower_part, preferred_element_type=jnp.float32
    )


def body(
    mix_input,
    state_write,
    state_read,
    log_decay,
    skip_gain,
    query_rows,
    key_rows,
    value_rows,
    incoming,
    norm_gain,
):
    tokens = mix_input.shape[1]
    heads_here = skip_gain.shape[0]
    width_here = mix_input.shape[2]
    head_size = width_here // heads_here
    narrow_inputs = mix_input[0].reshape(tokens, heads_here, head_size)
    inputs = narrow_inputs.astype(jnp.float32)
    decays = log_decay[0]
    cumulative = jnp.cumsum(decays, axis=0)
    write_rows = state_write[0]
    read_rows = state_read[0]
    pairing = jnp.dot(read_rows, write_rows.T, preferred_element_type=jnp.float32)
    token_positions = jnp.arange(tokens)
    causal = (token_positions[:, None] >= token_positions[None, :])[:, :, None]
    spread = cumulative[:, None, :] - cumulative[None, :, :]
    weights = jnp.where(causal, jnp.exp(jnp.where(causal, spread, 0.0)), 0.0) * pairing[:, :, None]
    inner_part = wide_first("tsh,shp->thp", weights, narrow_inputs)
    tail_decay = jnp.exp(cumulative[-1][None, :] - cumulative)
    local_state = wide_first("shp,sn->hpn", tail_decay[:, :, None] * inputs, write_rows)
    through = jnp.exp(cumulative[-1])
    neutral = (jnp.ones_like(through), jnp.zeros_like(local_state))
    entering = entering_2((through, local_state), "ctx", merge_states, neutral)[1]
    outer_part = jnp.exp(cumulative)[:, :, None] * wide_second("tn,hpn->thp", read_rows, entering)
    mixed_out = inner_part + outer_part + skip_gain[None, :, None] * inputs
    mamba_out = mixed_out.reshape(tokens, width_here).astype(jnp.bfloat16)
    onward = shifted(mamba_out, "pipe", 1)
    stream = jnp.where(lax.axis_index("pipe") == 0, incoming, onward)
    kv_here = key_rows.shape[2] // HEAD_DIM
    group_size = query_rows.shape[2] // (kv_here * HEAD_DIM)
    queries = query_rows[0].reshape(tokens, kv_here, group_size, HEAD_DIM)
    query_first = lax.axis_index("ctx") * tokens
    query_pos = query_first + token_positions
    inv_root = HEAD_DIM ** (-0.5)

    def attend_block(state_now, key_block, value_block, key_start):
        running_max, running_sum, weighted = state_now
        scores = (
            jnp.einsum("tgho,sgo->ghts", queries, key_block, preferred_element_type=jnp.float32)
            * inv_root
        )
        key_pos = key_start + jnp.arange(key_block.shape[0])
        allowed = key_pos[None, :] <= query_pos[:, None]
        masked = jnp.where(allowed, scores, -1e30)
        new_max = jnp.maximum(running_max, jnp.max(masked, axis=-1))
        softmax_terms = jnp.where(allowed, jnp.exp(masked - new_max[..., None]), 0.0)
        shrink = jnp.exp(running_max - new_max)
        running_sum = running_sum * shrink + jnp.sum(softmax_terms, axis=-1)
        weighted = weighted * shrink[..., None] + jnp.einsum(
            "ghts,sgo->ghto",
            softmax_terms.astype(jnp.bfloat16),
            value_block,
            preferred_element_type=jnp.float32,
        )
        return (new_max, running_sum, weighted)

    start_fold = (
        jnp.full((kv_here, group_size, tokens), -1e30, jnp.float32),
        jnp.zeros((kv_here, group_size, tokens), jnp.float32),
        jnp.zeros((kv_here, group_size, tokens, HEAD_DIM), jnp.float32),
    )
    key_piece = lax.all_gather(key_rows[0], "ctx", axis=0, tiled=True)
    value_piece = lax.all_gather(value_rows[0], "ctx", axis=0, tiled=True)
    piece_rows = key_piece.shape[0]
    block_rows = math.gcd(piece_rows, 512)
    block_count = piece_rows // block_rows
    key_blocks = key_piece.reshape(block_count, block_rows, kv_here, HEAD_DIM)
    value_blocks = value_piece.reshape(block_count, block_rows, kv_here, HEAD_DIM)
    block_starts = block_rows * jnp.arange(block_count)

    def advance_block(carried, blocks):
        return (attend_block(carried, blocks[0], blocks[1], blocks[2]), None)

    folded, _ = lax.scan(advance_block, start_fold, (key_blocks, value_blocks, block_starts))
    _, running_sum, weighted = folded
    heads_out = weighted / running_sum[..., None]
    attention = jnp.transpose(heads_out, (2, 0, 1, 3)).reshape(tokens, -1)
    summed = stream.astype(jnp.float32) + attention
    squares = lax.psum(jnp.sum(summed * summed, axis=1), "exp")
    scaled = summed * lax.rsqrt(squares / D + 1e-05)[:, None] * norm_gain[None, :]
    return (mamba_out[None], scaled.astype(jnp.bfloat16)[None])


def solution(mesh):
    placed = (
        P("pipe", "ctx", "exp"),
        P("pipe", "ctx", None),
        P("pipe", "ctx", None),
        P("pipe", "ctx", "exp"),
        P("exp"),
        P("pipe", "ctx", "exp"),
        P("pipe", "ctx", "exp"),
        P("pipe", "ctx", "exp"),
        P("ctx", "exp"),
        P("exp"),
    )
    return jax.shard_map(
        body,
        mesh=mesh,
        in_specs=placed,
        out_specs=(P("pipe", "ctx", "exp"), P("pipe", "ctx", "exp")),
        check_vma=False,
    )
```

profile of v0, /device:TPU:15, one launch (start us, length us, event | category | flops | bytes accessed | tf_op | source)
XLA Modules:
  0.0 122.2 jit_solution(14379086597654841328)
XLA Ops:
  7.2 0.0 copy-start
  7.2 0.0 all-gather.6.cloned.1.call-start
  7.2 0.8 copy.40
  8.1 0.2 reduce_window_sum.11
  8.3 0.1 copy.45
  8.4 1.6 %copy.43 = bf16[1,128,4096]{1,2,0:T(8,128)(2,1)S(1)} copy(bf16[1,128,4096]{2,1,0:T(8,128)(2,1)} %param.12) | data formatting | bytes 2097152 | tf_op args[0]
  10.0 0.0 copy-start.7
  10.0 0.3 subtract_convert_fusion.3
  10.4 0.4 copy-done.7
  10.7 0.4 fusion.32
  11.1 0.0 copy-start.6
  11.2 1.4 %add_convert_fusion = bf16[64,64,64]{2,1,0:T(8,128)(2,1)} fusion(f32[64,64,64]{2,1,0:T(8,128)S(1)} %fusion.32, bf16[128,64,64]{0,2,1:T(8,128)(2,1)S(1)} %bitcast.112, bf16[1,128,64]{1,2,0:T(8,128)(2,1)S(1)} %copy-done.7), kind=kOutput, calls=%fused_computation.24 | convolution fusion | flops 67633152 | bytes 2637824 | tf_op jit(solution)/shard_map/shp,sn->hpn/dot_general | solution.py:50
  12.5 0.0 all-gather.6.cloned.1.call-update
  12.6 0.1 copy.41
  12.6 4.9 %all-gather.3 = bf16[4,1,64]{2,1,0:T(2,128)(2,1)S(1)} all-gather(bf16[1,1,64]{2,1,0:T(2,128)(2,1)S(1)} %get-tuple-element.92), channel_id=1, replica_groups=mesh['pipe'=4,'ctx'=4,'exp'=2] {'ctx'}, dimensions={0}, use_global_device_ids=true | all-gather | bytes 640 | tf_op jit(solution)/shard_map/all_gather | solution.py:15
  17.6 0.1 copy.44
  17.6 0.0 copy-done.6
  17.7 0.2 copy.61
  17.9 0.1 copy.48
  18.0 11.7 %all-gather.1 = bf16[1,512,512]{1,2,0:T(8,128)(2,1)S(1)} all-gather(bf16[1,128,512]{1,2,0:T(8,128)(2,1)S(1)} %copy.48), channel_id=3, replica_groups=mesh['pipe'=4,'ctx'=4,'exp'=2] {'ctx'}, dimensions={1}, use_global_device_ids=true | all-gather | bytes 655360 | tf_op jit(solution)/shard_map/all_gather | solution.py:133
  29.8 2.0 %fusion = (f32[4,8,128]{2,1,0:T(8,128)S(1)}, f32[4,512,128,8]{2,1,3,0:T(8,128)S(1)}) fusion(pred[128,512]{0,1:T(8,128)(4,1)S(1)} %iota_compare_fusion, bf16[512,4,128,1]{0,2,3,1:T(8,128)(2,1)S(1)} %bitcast.113, bf16[128,4,8,128]{3,2,1,0:T(8,128)(2,1)S(1)} %bitcast.110), kind=kOutput, calls=%fused_computation.4 | convolution fusion | flops 543158272 | bytes 10043392 | tf_op jit(solution)/shard_map/while/body/eval_jaxpr/tgho,sgo->ghts/dot_general | solution.py:110
  31.9 0.0 copy-start.1
  31.9 0.2 fusion.34
  32.1 4.0 %fusion.19 = f32[64,128,64]{1,2,0:T(8,128)} fusion(bf16[128,64,64]{0,2,1:T(8,128)(2,1)S(1)} %bitcast.104, f32[128,128]{1,0:T(8,128)S(1)} %fusion.34, f32[128,64]{0,1:T(8,128)S(1)} %copy.41, pred[128,128]{1,0:T(8,128)(4,1)S(1)} %iota_compare_fusion.1), kind=kOutput, calls=%fused_computation.32 | convolution fusion | flops 139460608 | bytes 3260416 | tf_op jit(solution)/shard_map/tsh,shp->thp/dot_general | solution.py:50
  36.1 3.3 %fusion.7 = f32[64,128,64]{1,2,0:T(8,128)} fusion(bf16[128,64,64]{0,2,1:T(8,128)(2,1)S(1)} %bitcast.105, f32[128,128]{1,0:T(8,128)S(1)} %fusion.34, f32[128,64]{0,1:T(8,128)S(1)} %copy.41, pred[128,128]{1,0:T(8,128)(4,1)S(1)} %iota_compare_fusion.1), kind=kOutput, calls=%fused_computation.12 | convolution fusion | flops 142606336 | bytes 3260416 | tf_op jit(solution)/shard_map/tsh,shp->thp/dot_general | solution.py:50
  39.3 2.1 %fusion.1 = f32[4,8,128]{2,1,0:T(8,128)S(1)} fusion(f32[4,512,128,8]{2,1,3,0:T(8,128)S(1)} %get-tuple-element.96, f32[4,8,128]{2,1,0:T(8,128)S(1)} %get-tuple-element.94, pred[128,512]{0,1:T(8,128)(4,1)S(1)} %iota_compare_fusion), kind=kLoop, calls=%fused_computation.5 | loop fusion | flops 10481664 | bytes 8486912 | tf_op jit(solution)/shard_map/while/body/eval_jaxpr/reduce_sum | solution.py:119
  41.5 27.6 %all-gather.6.cloned.1.call-done = bf16[256,64,64]{2,1,0:T(8,128)(2,1)} async-done(((bf16[64,64,64]{2,1,0:T(8,128)(2,1)}), bf16[256,64,64]{2,1,0:T(8,128)(2,1)}) %all-gather.6.cloned.1.call-update) | async-done | bytes 2097168 | tf_op jit(solution)/shard_map/all_gather | solution.py:15
  69.1 0.2 broadcast_in_dim.72
  69.4 5.3 %while.3 = (s32[]{:T(128)}, f32[64,64,64]{2,1,0:T(8,128)S(1)}, s32[]{:T(128)}, bf16[4,64]{1,0:T(4,128)(2,1)S(1)}, bf16[4,64,64,64]{3,2,1,0:T(8,128)(2,1)}, /*index=5*/s32[]{:T(128)}, s32[]{:T(128)}, s32[]{:T(128)}) while((s32[]{:T(128)}, f32[64,64,64]{2,1,0:T(8,128)S(1)}, s32[]{:T(128)}, bf16[4,64]{1,0:T(4,128)(2,1)S(1)}, ...), condition=%wide.region_2.3_spmd, body=%wide.region_1.2_spmd.sunk | while | flops 786501 | bytes 2622207 | solution.py:29
  69.4 1.7 %convert_add_fusion.3 = f32[64,64,64]{2,1,0:T(8,128)S(1)} fusion(f32[64,64,64]{2,1,0:T(8,128)S(1)} %get-tuple-element.138, bf16[4,64,64,64]{3,2,1,0:T(8,128)(2,1)} %get-tuple-element.149, s32[]{:T(128)S(6)} %select_n.88, f32[64]{0:T(128)S(1)} %bitcast_convert_fusion.2), kind=kLoop, calls=%fused_computation.clone.1 | loop fusion | flops 786432 | bytes 2621700 | tf_op jit(solution)/shard_map/while/body/add | solution.py:39
  71.1 1.7 %convert_add_fusion.3 = f32[64,64,64]{2,1,0:T(8,128)S(1)} fusion(f32[64,64,64]{2,1,0:T(8,128)S(1)} %get-tuple-element.138, bf16[4,64,64,64]{3,2,1,0:T(8,128)(2,1)} %get-tuple-element.149, s32[]{:T(128)S(6)} %select_n.88, f32[64]{0:T(128)S(1)} %bitcast_convert_fusion.2), kind=kLoop, calls=%fused_computation.clone.1 | loop fusion | flops 786432 | bytes 2621700 | tf_op jit(solution)/shard_map/while/body/add | solution.py:39
  72.9 1.7 %convert_add_fusion.3 = f32[64,64,64]{2,1,0:T(8,128)S(1)} fusion(f32[64,64,64]{2,1,0:T(8,128)S(1)} %get-tuple-element.138, bf16[4,64,64,64]{3,2,1,0:T(8,128)(2,1)} %get-tuple-element.149, s32[]{:T(128)S(6)} %select_n.88, f32[64]{0:T(128)S(1)} %bitcast_convert_fusion.2), kind=kLoop, calls=%fused_computation.clone.1 | loop fusion | flops 786432 | bytes 2621700 | tf_op jit(solution)/shard_map/while/body/add | solution.py:39
  74.6 0.0 copy-start.11
  74.6 0.4 fusion.27
  75.1 1.1 copy-done.4
  76.2 0.6 copy-done.5
  76.8 1.9 %fusion.11 = bf16[128,64,64]{0,2,1:T(8,128)(2,1)} fusion(bf16[128,64,64]{0,2,1:T(8,128)(2,1)S(1)} %bitcast.106, f32[64,64,128]{2,1,0:T(8,128)S(1)} %fusion.27, f32[64,128,64]{1,2,0:T(8,128)S(1)} %copy-done.4, f32[64,128,64]{1,2,0:T(8,128)S(1)} %copy-done.5, f32[64,64,64]{2,1,0:T(8,128)S(1)} %get-tuple-element.70, f32[64]{0:T(128)S(1)} %copy-done.11, ...), kind=kOutput, calls=%fused_computation.18 | convolution fusion | flops 72351744 | bytes 9486592 | tf_op jit(solution)/shard_map/tn,hpn->thp/dot_general | solution.py:57
  78.7 2.3 %copy.47 = bf16[128,4096]{1,0:T(8,128)(2,1)} copy(bf16[128,4096]{0,1:T(8,128)(2,1)} %bitcast.107) | data formatting | bytes 2097152 | tf_op jit(solution)/shard_map/convert_element_type | solution.py:97
  81.0 3.1 %collective-permute-start = (bf16[128,4096]{1,0:T(8,128)(2,1)}, bf16[128,4096]{1,0:T(8,128)(2,1)}, u32[]{:S(2)}, u32[]{:S(2)}) collective-permute-start(bf16[128,4096]{1,0:T(8,128)(2,1)} %copy.47), channel_id=1, source_target_pairs={{0,8},{8,16},{16,24},{1,9},{9,17},{17,25},{2,10},{10,18},{18,26},{... | collective-permute-start | bytes 3145736 | tf_op jit(solution)/shard_map/ppermute | solution.py:35
  84.2 7.7 %all-gather.2 = bf16[1,512,512]{2,1,0:T(8,128)(2,1)S(1)} all-gather(bf16[1,128,512]{2,1,0:T(8,128)(2,1)S(1)} %copy-done.8), channel_id=4, replica_groups=mesh['pipe'=4,'ctx'=4,'exp'=2] {'ctx'}, dimensions={1}, use_global_device_ids=true | all-gather | bytes 655360 | tf_op jit(solution)/shard_map/all_gather | solution.py:134
  91.8 0.2 copy.51
  92.0 6.9 %fusion.8 = f32[128,4,8,128]{0,3,2,1:T(8,128)} fusion(bf16[512,4,128,1]{0,2,3,1:T(8,128)(2,1)S(1)} %bitcast.116, f32[4,512,128,8]{2,1,3,0:T(8,128)} %copy-done.1, f32[4,8,128]{2,1,0:T(8,128)S(1)} %get-tuple-element.94, pred[128,512]{0,1:T(8,128)(4,1)S(1)} %iota_compare_fusion, f32[128,4,8]{0,2,1:T(8,128)S(1)} %bitcast_add_fusion.1, ...), kind=kOutput, calls=%fused_computation.14 | convolution fusion | flops 548405248 | bytes 11124736 | tf_op jit(solution)/shard_map/while/body/eval_jaxpr/ghts,sgo->ghto/dot_general | solution.py:120
  99.0 2.0 %copy.53 = f32[128,4096]{1,0:T(8,128)S(1)} copy(f32[128,4096]{0,1:T(8,128)} %bitcast.114) | data formatting | bytes 4194304 | tf_op jit(solution)/shard_map/reshape | solution.py:148
  101.0 1.3 %copy.54 = bf16[1,128,4096]{2,1,0:T(8,128)(2,1)} copy(bf16[1,128,4096]{1,2,0:T(8,128)(2,1)S(1)} %bitcast.108) | data formatting | bytes 2097152
  102.3 4.9 %collective-permute-done = bf16[128,4096]{1,0:T(8,128)(2,1)} collective-permute-done((bf16[128,4096]{1,0:T(8,128)(2,1)}, bf16[128,4096]{1,0:T(8,128)(2,1)}, u32[]{:S(2)}, u32[]{:S(2)}) %collective-permute-start) | collective-permute-done | bytes 1048608 | tf_op jit(solution)/shard_map/ppermute | solution.py:35
  107.2 1.7 %multiply_reduce_fusion = f32[128]{0:T(128)S(1)} fusion(f32[128,4096]{1,0:T(8,128)S(1)} %copy.53, bf16[128,4096]{1,0:T(8,128)(2,1)} %param.20, bf16[128,4096]{1,0:T(8,128)(2,1)} %collective-permute-done, pred[]{:T(512)S(6)} %eq.3), kind=kLoop, calls=%fused_computation.21 | loop fusion | flops 2621312 | bytes 4194817 | tf_op jit(solution)/shard_map/reduce_sum | solution.py:150
  109.0 3.7 %psum.7 = f32[128]{0:T(128)S(1)} all-reduce(f32[128]{0:T(128)S(1)} %multiply_reduce_fusion), channel_id=1, replica_groups=mesh['pipe'=4,'ctx'=4,'exp'=2] {'exp'}, use_global_device_ids=true, to_apply=%region_6.7 | all-reduce | flops 128 | bytes 1024 | tf_op jit(solution)/shard_map/psum | solution.py:150
  112.7 2.7 %fusion.23 = bf16[1,128,4096]{2,1,0:T(8,128)(2,1)} fusion(f32[128,4096]{1,0:T(8,128)S(1)} %copy.53, f32[4096]{0:T(1024)S(1)} %copy-done.10, f32[128]{0:T(128)S(1)} %add_rsqrt_fusion, bf16[128,4096]{1,0:T(8,128)(2,1)S(1)} %copy-done.3, bf16[128,4096]{1,0:T(8,128)(2,1)} %collective-permute-done, pred[]{:T(512)S(6)} %eq.3), kind=kLoop, calls=%fused_computation.33 | loop fusion | flops 3145728 | bytes 5259777 | tf_op jit(solution)/shard_map/broadcast_in_dim | solution.py:152
  (27 shorter events, 0.2 us)
Async XLA Ops:
  7.2 24.7 %copy-start = (bf16[1,128,64]{1,2,0:T(8,128)(2,1)S(1)}, bf16[1,128,64]{1,2,0:T(8,128)(2,1)}, u32[]{:S(2)}) copy-start(bf16[1,128,64]{1,2,0:T(8,128)(2,1)} %param.14) | copy-start | bytes 49156
  7.2 61.9 %all-gather.6.cloned.1.call-start = ((), (), s32[]{:S(2)}) async-start(), calls=%async_computation | async-start | bytes 5242880 | tf_op jit(solution)/shard_map/all_gather | solution.py:15
  10.0 0.7 copy-start.7
  11.1 6.5 %copy-start.6 = (bf16[1,128,4096]{2,1,0:T(8,128)(2,1)S(1)}, bf16[1,128,4096]{2,1,0:T(8,128)(2,1)}, u32[]{:S(2)}) copy-start(bf16[1,128,4096]{2,1,0:T(8,128)(2,1)} %param.17) | copy-start | bytes 3145732
  12.5 5.4 %copy-start.9 = (bf16[1,128,512]{2,1,0:T(8,128)(2,1)S(1)}, bf16[1,128,512]{2,1,0:T(8,128)(2,1)}, u32[]{:S(2)}) copy-start(bf16[1,128,512]{2,1,0:T(8,128)(2,1)} %param.18) | copy-start | bytes 393220
  31.9 7.5 %copy-start.1 = (f32[4,512,128,8]{2,1,3,0:T(8,128)}, f32[4,512,128,8]{2,1,3,0:T(8,128)S(1)}, u32[]{:S(2)}) copy-start(f32[4,512,128,8]{2,1,3,0:T(8,128)S(1)} %get-tuple-element.96) | copy-start | bytes 25165828
  74.6 1.6 %copy-start.4 = (f32[64,128,64]{1,2,0:T(8,128)S(1)}, f32[64,128,64]{1,2,0:T(8,128)}, u32[]{:S(2)}) copy-start(f32[64,128,64]{1,2,0:T(8,128)} %fusion.19) | copy-start | bytes 6291460
  74.6 2.2 %copy-start.5 = (f32[64,128,64]{1,2,0:T(8,128)S(1)}, f32[64,128,64]{1,2,0:T(8,128)}, u32[]{:S(2)}) copy-start(f32[64,128,64]{1,2,0:T(8,128)} %fusion.7) | copy-start | bytes 6291460
  74.6 2.2 %copy-start.11 = (f32[64]{0:T(128)S(1)}, f32[64]{0:T(128)}, u32[]{:S(2)}) copy-start(f32[64]{0:T(128)} %param.16) | copy-start | bytes 772
  78.7 5.4 %copy-start.8 = (bf16[1,128,512]{2,1,0:T(8,128)(2,1)S(1)}, bf16[1,128,512]{2,1,0:T(8,128)(2,1)}, u32[]{:S(2)}) copy-start(bf16[1,128,512]{2,1,0:T(8,128)(2,1)} %param.19) | copy-start | bytes 393220
  81.0 26.2 %collective-permute-start = (bf16[128,4096]{1,0:T(8,128)(2,1)}, bf16[128,4096]{1,0:T(8,128)(2,1)}, u32[]{:S(2)}, u32[]{:S(2)}) collective-permute-start(bf16[128,4096]{1,0:T(8,128)(2,1)} %copy.47), channel_id=1, source_target_pairs={{0,8},{8,16},{16,24},{1,9},{9,17},{17,25},{2,10},{10,18},{18,26},{... | collective-permute-start | bytes 3145736 | tf_op jit(solution)/shard_map/ppermute | solution.py:35
  99.0 2.0 %copy-start.2 = (bf16[128,64,64]{0,2,1:T(8,128)(2,1)S(1)}, bf16[128,64,64]{0,2,1:T(8,128)(2,1)}, u32[]{:S(2)}) copy-start(bf16[128,64,64]{0,2,1:T(8,128)(2,1)} %fusion.11) | copy-start | bytes 3145732
  102.3 10.3 %copy-start.3 = (bf16[128,4096]{1,0:T(8,128)(2,1)S(1)}, bf16[128,4096]{1,0:T(8,128)(2,1)}, u32[]{:S(2)}) copy-start(bf16[128,4096]{1,0:T(8,128)(2,1)} %param.20) | copy-start | bytes 3145732
  102.3 10.3 %copy-start.10 = (f32[4096]{0:T(1024)S(1)}, f32[4096]{0:T(1024)}, u32[]{:S(2)}) copy-start(f32[4096]{0:T(1024)} %param.21) | copy-start | bytes 49156
Sparse Core Ops, SparseCore 0:
  12.7 56.3 all-gather.5
where the time goes:
time: 123 us; the launch traced here: 122 us
  waiting for transfers between devices  32.5 us (26%)
  blocking collectives  27.9 us (23%)
  matrix products  20.5 us (17%)
  between operations  14.3 us (12%)
  other arithmetic  12.3 us (10%)
  local copies, waits for them, and re-layouts  11.3 us (9%)
  starting transfers between devices  3.14 us (3%)
    all_gather x1, waiting for transfers between devices, entering_2(): lax.all_gather(a.astype(kind), axis)  27.6 us
    all_gather x1, blocking collectives, body(): key_piece = lax.all_gather(key_rows[0], 'ctx', axis=0, tiled=True)  11.7 us
    all_gather x1, blocking collectives, body(): value_piece = lax.all_gather(value_rows[0], 'ctx', axis=0, tiled=True)  7.66 us
    dot_general x1, matrix products, attend_block(): jnp.einsum('ghts,sgo->ghto', softmax_terms.astype(jnp.bfloat16), value_bl...  6.93 us
    unnamed x29, local copies, waits for them, and re-layouts  5.52 us
    add x3, other arithmetic, merge_states(): later[0][:, None, None] * earlier[1] + later[1]  5.11 us
    all_gather x1, blocking collectives, entering_2(): lax.all_gather(a.astype(kind), axis)  4.93 us
    ppermute x1, waiting for transfers between devices, shifted(): return lax.ppermute(block, axis, route)  4.93 us
  transfers between devices with their start and end apart: 2, of which 2 were waited for; matrix products, arithmetic and copies ran while one was open for 19% of the time, Pallas kernels for 0%

commit v1 on v0

v1 whole, which is shorter than its diff:
```python
import math

import jax
import jax.numpy as jnp
from jax import lax
from jax.experimental import pallas as pl
from jax.experimental.pallas import tpu as pltpu
from jax.sharding import PartitionSpec as P

D = 8192
HEAD_DIM = 128
LOG2E = 1.4426950408889634
F32 = jnp.float32
BF16 = jnp.bfloat16


def split_two(wide):
    upper = wide.astype(BF16)
    return upper, (wide - upper.astype(F32)).astype(BF16)


def dot32(a, b):
    return jnp.dot(a, b, preferred_element_type=F32)


def make_kernel(pipes, ranks, exps, tokens, heads, width, kv_width, nstate, chunk):
    size = width // heads
    chunks = width // chunk
    chunk_heads = chunk // size
    levels = ranks.bit_length() - 1
    kv_heads = kv_width // HEAD_DIM
    q_heads = width // HEAD_DIM
    group = q_heads // kv_heads
    together = math.gcd(4, group)
    keys = ranks * tokens

    def kernel(
        x_ref, write_ref, read_ref, decay_ref, skip_ref, q_ref, k_ref, v_ref, in_ref, gain_ref,
        mix_ref, out_ref,
        kbuf, vbuf, bias, stream, att, local, enter, outbox, inbox, spread_mat, cum_parts, cum_rows,
        pair_mat, dtot, dvec, tot_mine, tot_all, sq_mine, sq_all,
        st_send, st_recv, kv_send, kv_recv, tt_send, tt_recv, z_send, z_recv, e_send, e_recv,
    ):
        c = lax.axis_index("ctx")
        p = lax.axis_index("pipe")
        e = lax.axis_index("exp")

        def remote(src, dst, ssem, rsem, where):
            return pltpu.make_async_remote_copy(
                src_ref=src, dst_ref=dst, send_sem=ssem, recv_sem=rsem,
                device_id=where, device_id_type=pl.DeviceIdType.MESH,
            )

        barrier = pltpu.get_barrier_semaphore()
        for d in range(1, ranks):
            pl.semaphore_signal(barrier, inc=1, device_id={"ctx": lax.rem(c + d, ranks)},
                                device_id_type=pl.DeviceIdType.MESH)
        for d in range(1, exps):
            pl.semaphore_signal(barrier, inc=1, device_id={"exp": lax.rem(e + d, exps)},
                                device_id_type=pl.DeviceIdType.MESH)
        for d in (1, pipes - 1):
            pl.semaphore_signal(barrier, inc=1, device_id={"pipe": lax.rem(p + d, pipes)},
                                device_id_type=pl.DeviceIdType.MESH)

        rows = lax.broadcasted_iota(jnp.int32, (tokens, tokens), 0)
        cols = lax.broadcasted_iota(jnp.int32, (tokens, tokens), 1)
        tri = jnp.where(rows >= cols, 1.0, 0.0)
        cum = jnp.dot(tri, decay_ref[0] * LOG2E, precision=lax.Precision.HIGHEST,
                      preferred_element_type=F32)
        total = cum[tokens - 1:tokens, :]
        wide_cum = jnp.concatenate([cum, jnp.zeros((tokens, 128 - heads), F32)], axis=1)
        tot_mine[...] = jnp.broadcast_to(wide_cum[tokens - 1:tokens, :], tot_mine.shape)
        cum_rows[...] = jnp.transpose(wide_cum)
        for i in range(chunks):
            cum_parts[i] = wide_cum if i == 0 else pltpu.roll(wide_cum, 128 - i * chunk_heads, 1)
        spread_mat[...] = jnp.where(
            lax.broadcasted_iota(jnp.int32, (heads, width), 1) // size
            == lax.broadcasted_iota(jnp.int32, (heads, width), 0), 1.0, 0.0).astype(BF16)
        pairing = lax.dot_general(read_ref[0], write_ref[0], (((1,), (1,)), ((), ())),
                                  preferred_element_type=F32)
        pair_mat[...] = pairing * tri
        tail = split_two(jnp.exp2(total - cum))
        since = split_two(jnp.exp2(cum))
        skips = split_two(jnp.broadcast_to(skip_ref[...], (8, heads)))
        write_t = jnp.transpose(write_ref[0].astype(F32)).astype(BF16)

        pl.semaphore_wait(barrier, ranks - 1 + exps - 1 + 2)

        def tot_copy(d):
            return remote(tot_mine, tot_all.at[c], tt_send.at[d], tt_recv.at[c], {"ctx": c + d})

        for d in range(1, ranks):
            @pl.when(c + d < ranks)
            def _():
                tot_copy(d).start()

        def state_copy(level, d, i):
            at = pl.ds(pl.multiple_of(i * chunk, chunk), chunk)
            return remote(outbox.at[:, at], inbox.at[level, :, at], st_send.at[d, i],
                          st_recv.at[level, i], {"ctx": c + 1 + d})

        def sends_at(level):
            return lax.rem(c, 2 ** (level + 1)) == 2 ** level - 1

        def make_local(i, _):
            at = pl.ds(pl.multiple_of(i * chunk, chunk), chunk)
            mat = spread_mat[:, at]
            scaled = (dot32(tail[0], mat) + dot32(tail[1], mat)) * x_ref[0, :, at].astype(F32)
            state = dot32(write_t, scaled.astype(BF16))
            local[:, at] = state

            @pl.when(lax.rem(c, 2) == 0)
            def _():
                outbox[:, at] = state.astype(BF16)
                state_copy(0, 0, i).start()
            return 0

        lax.fori_loop(0, chunks, make_local, 0)

        def kv_copies(d):
            where = {"ctx": c + d}
            return (
                remote(k_ref.at[0], kbuf.at[c], kv_send.at[d, 0], kv_recv.at[c, 0], where),
                remote(v_ref.at[0], vbuf.at[c], kv_send.at[d, 1], kv_recv.at[c, 1], where),
            )

        for d in range(1, ranks):
            @pl.when(c + d < ranks)
            def _():
                for copy in kv_copies(d):
                    copy.start()

        for d in range(1, ranks):
            @pl.when(c >= d)
            def _():
                remote(tot_mine, tot_all.at[c - d], tt_send.at[d], tt_recv.at[c - d],
                       {"ctx": c}).wait_recv()
        def expand_row(logs):
            parts = split_two(jnp.exp2(logs)[:, :heads])
            return dot32(parts[0], spread_mat[...]) + dot32(parts[1], spread_mat[...])

        dtot[0] = expand_row(tot_mine[...])
        dtot[1] = dot32(skips[0], spread_mat[...]) + dot32(skips[1], spread_mat[...])
        for level in range(1, levels):
            base = (c // 2 ** level) * 2 ** level
            logs = jnp.zeros((8, 128), F32)
            for j in range(ranks):
                logs = logs + jnp.where((j >= base) & (j < c), tot_all[j], 0.0)
            dvec[level] = expand_row(logs)

        def receive(i):
            at = pl.ds(pl.multiple_of(i * chunk, chunk), chunk)
            enter[:, at] = jnp.zeros((nstate, chunk), F32)
            for level in range(levels):
                @pl.when(lax.rem(c // 2 ** level, 2) == 1)
                def _():
                    state_copy(level, 0, i).wait_recv()
                    got = inbox[level, :, at].astype(F32)
                    if level > 0:
                        got = dvec[level, 0:1, at] * got
                    enter[:, at] = enter[:, at] + got

        forwards = (lax.rem(c, 2) == 1) & (c < ranks - 1)

        @pl.when(forwards)
        def _():
            def forward(i, _):
                at = pl.ds(pl.multiple_of(i * chunk, chunk), chunk)
                receive(i)
                outbox[:, at] = (dtot[0, 0:1, at] * enter[:, at] + local[:, at]).astype(BF16)
                for level in range(1, levels):
                    @pl.when(sends_at(level))
                    def _():
                        for d in range(2 ** level):
                            state_copy(level, d, i).start()
                return 0
            lax.fori_loop(0, chunks, forward, 0)

        def onward(i):
            at = pl.ds(pl.multiple_of(i * chunk, chunk), chunk)
            return remote(mix_ref.at[0, :, at], stream.at[:, at], z_send.at[i], z_recv.at[i],
                          {"pipe": p + 1})

        lane = lax.broadcasted_iota(jnp.int32, (tokens, 2 * size), 1)

        def finish_mix(i, _):
            at = pl.ds(pl.multiple_of(i * chunk, chunk), chunk)

            @pl.when(jnp.logical_not(forwards))
            def _():
                receive(i)

            mat = spread_mat[:, at]
            grown = dot32(since[0], mat) + dot32(since[1], mat)
            outer = grown * dot32(read_ref[0], enter[:, at].astype(BF16))
            outer = outer + dtot[1, 0:1, at] * x_ref[0, :, at].astype(F32)
            columns = cum_parts[i]
            lines = cum_rows[pl.ds(pl.multiple_of(i * chunk_heads, chunk_heads), chunk_heads), :]
            inner = []
            for k in range(0, chunk_heads, 2):
                both = []
                for h in (k, k + 1):
                    spread = jnp.minimum(columns[:, h:h + 1] - lines[h:h + 1, :], 0.0)
                    both.append((jnp.exp2(spread) * pair_mat[...]).astype(BF16))
                start = pl.multiple_of(i * chunk + k * size, 2 * size)
                xs = x_ref[0, :, pl.ds(start, 2 * size)]
                zero = jnp.zeros_like(xs)
                halves = jnp.concatenate(
                    [jnp.where(lane < size, xs, zero), jnp.where(lane < size, zero, xs)], axis=0)
                inner.append(dot32(jnp.concatenate(both, axis=1), halves))
            mix_ref[0, :, at] = (jnp.concatenate(inner, axis=1) + outer).astype(BF16)

            @pl.when(p < pipes - 1)
            def _():
                onward(i).start()
            return 0

        lax.fori_loop(0, chunks, finish_mix, 0)

        @pl.when(p == 0)
        def _():
            stream[...] = in_ref[...]

        kbuf[c] = k_ref[0]
        vbuf[c] = v_ref[0]
        for j in range(1, ranks):
            @pl.when(j > c)
            def _():
                kbuf[j] = jnp.zeros(kbuf.shape[1:], BF16)
                vbuf[j] = jnp.zeros(vbuf.shape[1:], BF16)
        bias[...] = jnp.where(
            lax.broadcasted_iota(jnp.int32, (tokens, keys), 1)
            <= c * tokens + lax.broadcasted_iota(jnp.int32, (tokens, keys), 0), 0.0, -1e30)
        for d in range(1, ranks):
            @pl.when(c >= d)
            def _():
                where = {"ctx": c}
                remote(k_ref.at[0], kbuf.at[c - d], kv_send.at[d, 0], kv_recv.at[c - d, 0], where).wait_recv()
                remote(v_ref.at[0], vbuf.at[c - d], kv_send.at[d, 1], kv_recv.at[c - d, 1], where).wait_recv()

        def attend(step, _):
            for r in range(together):
                h = step * together + r
                at = pl.ds(pl.multiple_of(h * HEAD_DIM, HEAD_DIM), HEAD_DIM)
                g = (step * together) // group
                kv_at = pl.ds(pl.multiple_of(g * HEAD_DIM, HEAD_DIM), HEAD_DIM)
                kk = kbuf[:, :, kv_at].reshape(keys, HEAD_DIM)
                vv = vbuf[:, :, kv_at].reshape(keys, HEAD_DIM)
                s = lax.dot_general(q_ref[0, :, at], kk, (((1,), (1,)), ((), ())),
                                    preferred_element_type=F32)
                s = s * (LOG2E * HEAD_DIM ** -0.5) + bias[...]
                terms = jnp.exp2(s - jnp.max(s, axis=1, keepdims=True))
                weighted = dot32(terms.astype(BF16), vv)
                att[:, at] = weighted * (1.0 / jnp.sum(terms, axis=1, keepdims=True))
            return 0

        lax.fori_loop(0, q_heads // together, attend, 0)

        sq_mine[...] = jnp.zeros_like(sq_mine)

        def add_up(i, _):
            at = pl.ds(pl.multiple_of(i * chunk, chunk), chunk)

            @pl.when(p > 0)
            def _():
                onward(i).wait_recv()
            summed = stream[:, at].astype(F32) + att[:, at]
            att[:, at] = summed
            square = summed * summed
            part = square[:, :128]
            for k in range(1, chunk // 128):
                part = part + square[:, k * 128:(k + 1) * 128]
            sq_mine[...] += part
            return 0

        lax.fori_loop(0, chunks, add_up, 0)
        swaps = [
            remote(sq_mine, sq_all.at[d - 1], e_send.at[d - 1], e_recv.at[d - 1],
                   {"exp": lax.rem(e + d, exps)})
            for d in range(1, exps)
        ]
        for copy in swaps:
            copy.start()
        for copy in swaps:
            copy.wait()
        squares = sq_mine[...]
        for d in range(exps - 1):
            squares = squares + sq_all[d]
        factor = lax.rsqrt(jnp.sum(squares, axis=1, keepdims=True) / D + 1e-05)

        def scale(i, _):
            at = pl.ds(pl.multiple_of(i * chunk, chunk), chunk)
            out_ref[0, :, at] = (att[:, at] * factor * gain_ref[0:1, at]).astype(BF16)
            return 0

        lax.fori_loop(0, chunks, scale, 0)

        for d in range(1, ranks):
            @pl.when(c + d < ranks)
            def _():
                tot_copy(d).wait_send()
                for copy in kv_copies(d):
                    copy.wait_send()
        for level in range(levels):
            @pl.when(sends_at(level))
            def _():
                def drain(i, _):
                    for d in range(2 ** level):
                        state_copy(level, d, i).wait_send()
                    return 0
                lax.fori_loop(0, chunks, drain, 0)

        @pl.when(p < pipes - 1)
        def _():
            def drain(i, _):
                onward(i).wait_send()
                return 0
            lax.fori_loop(0, chunks, drain, 0)

    scratch = [
        pltpu.VMEM((ranks, tokens, kv_width), BF16),
        pltpu.VMEM((ranks, tokens, kv_width), BF16),
        pltpu.VMEM((tokens, keys), F32),
        pltpu.VMEM((tokens, width), BF16),
        pltpu.VMEM((tokens, width), F32),
        pltpu.VMEM((nstate, width), F32),
        pltpu.VMEM((nstate, width), F32),
        pltpu.VMEM((nstate, width), BF16),
        pltpu.VMEM((levels, nstate, width), BF16),
        pltpu.VMEM((heads, width), BF16),
        pltpu.VMEM((chunks, tokens, 128), F32),
        pltpu.VMEM((128, tokens), F32),
        pltpu.VMEM((tokens, tokens), F32),
        pltpu.VMEM((2, 8, width), F32),
        pltpu.VMEM((levels, 8, width), F32),
        pltpu.VMEM((8, 128), F32),
        pltpu.VMEM((ranks, 8, 128), F32),
        pltpu.VMEM((tokens, 128), F32),
        pltpu.VMEM((max(exps - 1, 1), tokens, 128), F32),
        pltpu.SemaphoreType.DMA((ranks // 2, chunks)),
        pltpu.SemaphoreType.DMA((levels, chunks)),
        pltpu.SemaphoreType.DMA((ranks, 2)),
        pltpu.SemaphoreType.DMA((ranks, 2)),
        pltpu.SemaphoreType.DMA((ranks,)),
        pltpu.SemaphoreType.DMA((ranks,)),
        pltpu.SemaphoreType.DMA((chunks,)),
        pltpu.SemaphoreType.DMA((chunks,)),
        pltpu.SemaphoreType.DMA((exps,)),
        pltpu.SemaphoreType.DMA((exps,)),
    ]
    return kernel, scratch


def solution(mesh):
    pipes, ranks, exps = (mesh.shape[a] for a in ("pipe", "ctx", "exp"))

    def body(
        mix_input, state_write, state_read, log_decay, skip_gain, query_rows, key_rows,
        value_rows, incoming, norm_gain,
    ):
        tokens, width = mix_input.shape[1:]
        heads = skip_gain.shape[0]
        kernel, scratch = make_kernel(
            pipes, ranks, exps, tokens, heads, width, key_rows.shape[2], state_write.shape[2], 512)
        vmem = pl.BlockSpec(memory_space=pltpu.VMEM)
        shape = jax.ShapeDtypeStruct(mix_input.shape, BF16)
        return pl.pallas_call(
            kernel,
            out_shape=(shape, shape),
            in_specs=[vmem] * 10,
            out_specs=(vmem, vmem),
            scratch_shapes=scratch,
            compiler_params=pltpu.CompilerParams(
                collective_id=0, has_side_effects=True, vmem_limit_bytes=48 * 2 ** 20),
        )(mix_input, state_write, state_read, log_decay, skip_gain[None], query_rows, key_rows,
          value_rows, incoming, norm_gain[None])

    placed = (
        P("pipe", "ctx", "exp"), P("pipe", "ctx", None), P("pipe", "ctx", None),
        P("pipe", "ctx", "exp"), P("exp"), P("pipe", "ctx", "exp"), P("pipe", "ctx", "exp"),
        P("pipe", "ctx", "exp"), P("ctx", "exp"), P("exp"),
    )
    return jax.shard_map(
        body, mesh=mesh, in_specs=placed,
        out_specs=(P("pipe", "ctx", "exp"), P("pipe", "ctx", "exp")), check_vma=False,
    )
```

time: 123 us -> 52.9 us (0.43)
  the two profiles are of different devices: /device:TPU:15 before, /device:TPU:7 now
where the time goes in v1:
time: 52.9 us; the launch traced here: 52.5 us
  Pallas kernels  42.8 us (81%)
  local copies, waits for them, and re-layouts  9.09 us (17%)
  between operations  0.71 us (1%)
    pallas_call x1, Pallas kernels, body(): pl.pallas_call(kernel, out_shape=(shape, shape), in_specs=[vmem] * 10, ou...  42.8 us
    unnamed x19, local copies, waits for them, and re-layouts  9.09 us

profile of v1, /device:TPU:7, one launch (start us, length us, event | category | flops | bytes accessed | tf_op | source)
XLA Modules:
  0.0 52.5 jit_solution(3330156051873668695)
XLA Ops:
  0.6 0.0 copy-start.3
  0.6 0.9 %copy.12.write_ref = bf16[1,128,64]{2,1,0:T(8,128)(2,1)S(1)} copy(bf16[1,128,64]{1,2,0:T(8,128)(2,1)} %param.11) | data formatting | bytes 32768 | tf_op args[1]
  1.5 0.8 %copy.13.read_ref = bf16[1,128,64]{2,1,0:T(8,128)(2,1)S(1)} copy(bf16[1,128,64]{1,2,0:T(8,128)(2,1)} %param.12) | data formatting | bytes 32768 | tf_op args[2]
  2.3 0.0 copy-start.5
  2.3 0.0 copy-start.6
  2.4 0.9 %copy.14.decay_ref = f32[1,128,64]{2,1,0:T(8,128)S(1)} copy(f32[1,128,64]{1,2,0:T(8,128)} %param.13) | data formatting | bytes 65536 | tf_op args[3]
  3.2 0.0 copy-done.3
  3.2 0.0 copy-done.5
  3.3 0.0 copy-done.6
  3.3 0.0 copy-start
  3.3 1.2 %copy-done = bf16[1,128,4096]{2,1,0:T(8,128)(2,1)S(1)} copy-done((bf16[1,128,4096]{2,1,0:T(8,128)(2,1)S(1)}, bf16[1,128,4096]{2,1,0:T(8,128)(2,1)}, u32[]{:S(2)}) %copy-start) | copy-done | bytes 1048600
  4.5 0.0 copy-start.1
  4.5 1.2 %copy-done.1 = bf16[1,128,4096]{2,1,0:T(8,128)(2,1)S(1)} copy-done((bf16[1,128,4096]{2,1,0:T(8,128)(2,1)S(1)}, bf16[1,128,4096]{2,1,0:T(8,128)(2,1)}, u32[]{:S(2)}) %copy-start.1) | copy-done | bytes 1048600
  5.7 0.0 copy-start.2
  5.7 1.2 %copy-done.2 = bf16[128,4096]{1,0:T(8,128)(2,1)S(1)} copy-done((bf16[128,4096]{1,0:T(8,128)(2,1)S(1)}, bf16[128,4096]{1,0:T(8,128)(2,1)}, u32[]{:S(2)}) %copy-start.2) | copy-done | bytes 1048600
  6.9 0.0 copy-start.4
  6.9 0.9 %copy-done.4 = bf16[1,128,512]{2,1,0:T(8,128)(2,1)S(1)} copy-done((bf16[1,128,512]{2,1,0:T(8,128)(2,1)S(1)}, bf16[1,128,512]{2,1,0:T(8,128)(2,1)}, u32[]{:S(2)}) %copy-start.4) | copy-done | bytes 131096
  7.8 42.8 %shard_map.113 = (bf16[1,128,4096]{2,1,0:T(8,128)(2,1)S(1)}, bf16[1,128,4096]{2,1,0:T(8,128)(2,1)S(1)}) custom-call(bf16[1,128,4096]{2,1,0:T(8,128)(2,1)S(1)} %copy-done, bf16[1,128,64]{2,1,0:T(8,128)(2,1)S(1)} %copy.12.write_ref, bf16[1,128,64]{2,1,0:T(8,128)(2,1)S(1)} %copy.13.read_ref, f32[1,128,64]{2,1,0:T(8,128)S(1)} %copy.14.decay_ref, ...), custom_call_target="tpu_custom_call" | custom-call | tf_op jit(solution)/shard_map/pallas_call | solution.py:367
  50.6 1.0 %copy.17 = bf16[1,128,4096]{2,1,0:T(8,128)(2,1)} copy(bf16[1,128,4096]{2,1,0:T(8,128)(2,1)S(1)} %get-tuple-element.4) | data formatting | bytes 2097152
  51.6 1.0 %copy.18 = bf16[1,128,4096]{2,1,0:T(8,128)(2,1)} copy(bf16[1,128,4096]{2,1,0:T(8,128)(2,1)S(1)} %get-tuple-element.5) | data formatting | bytes 2097152
Async XLA Ops:
  0.6 2.6 %copy-start.3 = (bf16[1,128,512]{2,1,0:T(8,128)(2,1)S(1)}, bf16[1,128,512]{2,1,0:T(8,128)(2,1)}, u32[]{:S(2)}) copy-start(bf16[1,128,512]{2,1,0:T(8,128)(2,1)} %k_ref.1) | copy-start | bytes 393220
  2.3 0.9 %copy-start.5 = (f32[4096]{0:T(1024)S(1)}, f32[4096]{0:T(1024)}, u32[]{:S(2)}) copy-start(f32[4096]{0:T(1024)} %param.19) | copy-start | bytes 49156
  2.3 0.9 %copy-start.6 = (f32[64]{0:T(128)S(1)}, f32[64]{0:T(128)}, u32[]{:S(2)}) copy-start(f32[64]{0:T(128)} %param.14) | copy-start | bytes 772
  3.3 1.2 %copy-start = (bf16[1,128,4096]{2,1,0:T(8,128)(2,1)S(1)}, bf16[1,128,4096]{2,1,0:T(8,128)(2,1)}, u32[]{:S(2)}) copy-start(bf16[1,128,4096]{2,1,0:T(8,128)(2,1)} %x_ref.1) | copy-start | bytes 3145732
  4.5 1.2 %copy-start.1 = (bf16[1,128,4096]{2,1,0:T(8,128)(2,1)S(1)}, bf16[1,128,4096]{2,1,0:T(8,128)(2,1)}, u32[]{:S(2)}) copy-start(bf16[1,128,4096]{2,1,0:T(8,128)(2,1)} %q_ref.1) | copy-start | bytes 3145732
  5.7 1.2 %copy-start.2 = (bf16[128,4096]{1,0:T(8,128)(2,1)S(1)}, bf16[128,4096]{1,0:T(8,128)(2,1)}, u32[]{:S(2)}) copy-start(bf16[128,4096]{1,0:T(8,128)(2,1)} %in_ref.1) | copy-start | bytes 3145732
  6.9 0.9 %copy-start.4 = (bf16[1,128,512]{2,1,0:T(8,128)(2,1)S(1)}, bf16[1,128,512]{2,1,0:T(8,128)(2,1)}, u32[]{:S(2)}) copy-start(bf16[1,128,512]{2,1,0:T(8,128)(2,1)} %v_ref.1) | copy-start | bytes 393220

commit v2 on v1

--- a/solution.py
+++ b/solution.py
@@ -1,5 +1,3 @@
-import math
-
 import jax
 import jax.numpy as jnp
 from jax import lax
@@ -30,13 +28,12 @@
     levels = ranks.bit_length() - 1
     kv_heads = kv_width // HEAD_DIM
     q_heads = width // HEAD_DIM
-    group = q_heads // kv_heads
-    together = math.gcd(4, group)
     keys = ranks * tokens
 
     def kernel(
-        x_ref, write_ref, read_ref, decay_ref, skip_ref, q_ref, k_ref, v_ref, in_ref, gain_ref,
+        x_hbm, write_hbm, read_hbm, decay_hbm, skip_hbm, q_hbm, k_hbm, v_hbm, in_hbm, gain_hbm,
         mix_ref, out_ref,
+        x_ref, write_ref, read_ref, decay_ref, skip_ref, q_ref, gain_ref, in_sem, x_sem, kv_sem,
         kbuf, vbuf, bias, stream, att, local, enter, outbox, inbox, spread_mat, cum_parts, cum_rows,
         pair_mat, dtot, dvec, tot_mine, tot_all, sq_mine, sq_all,
         st_send, st_recv, kv_send, kv_recv, tt_send, tt_recv, z_send, z_recv, e_send, e_recv,
@@ -50,6 +47,37 @@
                 src_ref=src, dst_ref=dst, send_sem=ssem, recv_sem=rsem,
                 device_id=where, device_id_type=pl.DeviceIdType.MESH,
             )
+
+        small = [
+            pltpu.make_async_copy(src, dst, in_sem.at[i])
+            for i, (src, dst) in enumerate((
+                (decay_hbm.at[0], decay_ref), (write_hbm.at[0], write_ref),
+                (read_hbm.at[0], read_ref), (skip_hbm, skip_ref), (gain_hbm, gain_ref)))
+        ]
+        for copy in small:
+            copy.start()
+
+        def own_kv(g):
+            at = pl.ds(pl.multiple_of(g * HEAD_DIM, HEAD_DIM), HEAD_DIM)
+            return (pltpu.make_async_copy(k_hbm.at[0, :, at], kbuf.at[c, g], kv_sem.at[g, 0]),
+                    pltpu.make_async_copy(v_hbm.at[0, :, at], vbuf.at[c, g], kv_sem.at[g, 1]))
+
+        def own_x(i):
+            at = pl.ds(pl.multiple_of(i * chunk, chunk), chunk)
+            return pltpu.make_async_copy(x_hbm.at[0, :, at], x_ref.at[:, at], x_sem.at[i])
+
+        for g in range(kv_heads):
+            for copy in own_kv(g):
+                copy.start()
+        for i in range(chunks):
+            own_x(i).start()
+        q_copy = pltpu.make_async_copy(q_hbm.at[0], q_ref, in_sem.at[5])
+        q_copy.start()
+        in_copy = pltpu.make_async_copy(in_hbm, stream, in_sem.at[6])
+
+        @pl.when(p == 0)
+        def _():
+            in_copy.start()
 
         barrier = pltpu.get_barrier_semaphore()
         for d in range(1, ranks):
@@ -65,24 +93,26 @@
         rows = lax.broadcasted_iota(jnp.int32, (tokens, tokens), 0)
         cols = lax.broadcasted_iota(jnp.int32, (tokens, tokens), 1)
         tri = jnp.where(rows >= cols, 1.0, 0.0)
-        cum = jnp.dot(tri, decay_ref[0] * LOG2E, precision=lax.Precision.HIGHEST,
-                      preferred_element_type=F32)
+        spread_mat[...] = jnp.where(
+            lax.broadcasted_iota(jnp.int32, (heads, width), 1) // size
+            == lax.broadcasted_iota(jnp.int32, (heads, width), 0), 1.0, 0.0).astype(BF16)
+        for copy in small:
+            copy.wait()
+        by_token = jnp.transpose(jnp.concatenate(
+            [decay_ref[...] * LOG2E, jnp.zeros((128 - heads, tokens), F32)], axis=0))
+        wide_cum = jnp.dot(tri, by_token, precision=lax.Precision.HIGHEST,
+                           preferred_element_type=F32)
+        cum = wide_cum[:, :heads]
         total = cum[tokens - 1:tokens, :]
-        wide_cum = jnp.concatenate([cum, jnp.zeros((tokens, 128 - heads), F32)], axis=1)
         tot_mine[...] = jnp.broadcast_to(wide_cum[tokens - 1:tokens, :], tot_mine.shape)
         cum_rows[...] = jnp.transpose(wide_cum)
         for i in range(chunks):
             cum_parts[i] = wide_cum if i == 0 else pltpu.roll(wide_cum, 128 - i * chunk_heads, 1)
-        spread_mat[...] = jnp.where(
-            lax.broadcasted_iota(jnp.int32, (heads, width), 1) // size
-            == lax.broadcasted_iota(jnp.int32, (heads, width), 0), 1.0, 0.0).astype(BF16)
-        pairing = lax.dot_general(read_ref[0], write_ref[0], (((1,), (1,)), ((), ())),
-                                  preferred_element_type=F32)
-        pair_mat[...] = pairing * tri
+        read_rows = jnp.transpose(read_ref[...].astype(F32)).astype(BF16)
+        pair_mat[...] = dot32(read_rows, write_ref[...]) * tri
         tail = split_two(jnp.exp2(total - cum))
         since = split_two(jnp.exp2(cum))
         skips = split_two(jnp.broadcast_to(skip_ref[...], (8, heads)))
-        write_t = jnp.transpose(write_ref[0].astype(F32)).astype(BF16)
 
         pl.semaphore_wait(barrier, ranks - 1 + exps - 1 + 2)
 
@@ -102,33 +132,45 @@
         def sends_at(level):
             return lax.rem(c, 2 ** (level + 1)) == 2 ** level - 1
 
+        def kv_copies(d, g):
+            where = {"ctx": c + d}
+            return (
+                remote(kbuf.at[c, g], kbuf.at[c, g], kv_send.at[d, g, 0], kv_recv.at[c, g, 0], where),
+                remote(vbuf.at[c, g], vbuf.at[c, g], kv_send.at[d, g, 1], kv_recv.at[c, g, 1], where),
+            )
+
+        def wait_kv(d, g):
+            where = {"ctx": c}
+            j = c - d
+            remote(kbuf.at[j, g], kbuf.at[j, g], kv_send.at[d, g, 0], kv_recv.at[j, g, 0], where).wait_recv()
+            remote(vbuf.at[j, g], vbuf.at[j, g], kv_send.at[d, g, 1], kv_recv.at[j, g, 1], where).wait_recv()
+
         def make_local(i, _):
             at = pl.ds(pl.multiple_of(i * chunk, chunk), chunk)
+            own_x(i).wait()
             mat = spread_mat[:, at]
-            scaled = (dot32(tail[0], mat) + dot32(tail[1], mat)) * x_ref[0, :, at].astype(F32)
-            state = dot32(write_t, scaled.astype(BF16))
+            scaled = (dot32(tail[0], mat) + dot32(tail[1], mat)) * x_ref[:, at].astype(F32)
+            state = dot32(write_ref[...], scaled.astype(BF16))
             local[:, at] = state
 
             @pl.when(lax.rem(c, 2) == 0)
             def _():
                 outbox[:, at] = state.astype(BF16)
                 state_copy(0, 0, i).start()
+
+            @pl.when(lax.rem(i, chunks // kv_heads) == 0)
+            def _():
+                g = i // (chunks // kv_heads)
+                for copy in own_kv(g):
+                    copy.wait()
+                for d in range(1, ranks):
+                    @pl.when(c + d < ranks)
+                    def _():
+                        for copy in kv_copies(d, g):
+                            copy.start()
             return 0
 
         lax.fori_loop(0, chunks, make_local, 0)
-
-        def kv_copies(d):
-            where = {"ctx": c + d}
-            return (
-                remote(k_ref.at[0], kbuf.at[c], kv_send.at[d, 0], kv_recv.at[c, 0], where),
-                remote(v_ref.at[0], vbuf.at[c], kv_send.at[d, 1], kv_recv.at[c, 1], where),
-            )
-
-        for d in range(1, ranks):
-            @pl.when(c + d < ranks)
-            def _():
-                for copy in kv_copies(d):
-                    copy.start()
 
         for d in range(1, ranks):
             @pl.when(c >= d)
@@ -162,38 +204,31 @@
 
         forwards = (lax.rem(c, 2) == 1) & (c < ranks - 1)
 
-        @pl.when(forwards)
-        def _():
-            def forward(i, _):
-                at = pl.ds(pl.multiple_of(i * chunk, chunk), chunk)
-                receive(i)
+        def onward(i):
+            at = pl.ds(pl.multiple_of(i * chunk, chunk), chunk)
+            return remote(mix_ref.at[0, :, at], stream.at[:, at], z_send.at[i], z_recv.at[i],
+                          {"pipe": p + 1})
+
+        lane = lax.broadcasted_iota(jnp.int32, (tokens, 2 * size), 1)
+
+        def finish_mix(i, _):
+            at = pl.ds(pl.multiple_of(i * chunk, chunk), chunk)
+
+            receive(i)
+
+            @pl.when(forwards)
+            def _():
                 outbox[:, at] = (dtot[0, 0:1, at] * enter[:, at] + local[:, at]).astype(BF16)
                 for level in range(1, levels):
                     @pl.when(sends_at(level))
                     def _():
                         for d in range(2 ** level):
                             state_copy(level, d, i).start()
-                return 0
-            lax.fori_loop(0, chunks, forward, 0)
-
-        def onward(i):
-            at = pl.ds(pl.multiple_of(i * chunk, chunk), chunk)
-            return remote(mix_ref.at[0, :, at], stream.at[:, at], z_send.at[i], z_recv.at[i],
-                          {"pipe": p + 1})
-
-        lane = lax.broadcasted_iota(jnp.int32, (tokens, 2 * size), 1)
-
-        def finish_mix(i, _):
-            at = pl.ds(pl.multiple_of(i * chunk, chunk), chunk)
-
-            @pl.when(jnp.logical_not(forwards))
-            def _():
-                receive(i)
 
             mat = spread_mat[:, at]
             grown = dot32(since[0], mat) + dot32(since[1], mat)
-            outer = grown * dot32(read_ref[0], enter[:, at].astype(BF16))
-            outer = outer + dtot[1, 0:1, at] * x_ref[0, :, at].astype(F32)
+            outer = grown * dot32(read_rows, enter[:, at].astype(BF16))
+            outer = outer + dtot[1, 0:1, at] * x_ref[:, at].astype(F32)
             columns = cum_parts[i]
             lines = cum_rows[pl.ds(pl.multiple_of(i * chunk_heads, chunk_heads), chunk_heads), :]
             inner = []
@@ -203,7 +238,7 @@
                     spread = jnp.minimum(columns[:, h:h + 1] - lines[h:h + 1, :], 0.0)
                     both.append((jnp.exp2(spread) * pair_mat[...]).astype(BF16))
                 start = pl.multiple_of(i * chunk + k * size, 2 * size)
-                xs = x_ref[0, :, pl.ds(start, 2 * size)]
+                xs = x_ref[:, pl.ds(start, 2 * size)]
                 zero = jnp.zeros_like(xs)
                 halves = jnp.concatenate(
                     [jnp.where(lane < size, xs, zero), jnp.where(lane < size, zero, xs)], axis=0)
@@ -215,14 +250,6 @@
                 onward(i).start()
             return 0
 
-        lax.fori_loop(0, chunks, finish_mix, 0)
-
-        @pl.when(p == 0)
-        def _():
-            stream[...] = in_ref[...]
-
-        kbuf[c] = k_ref[0]
-        vbuf[c] = v_ref[0]
         for j in range(1, ranks):
             @pl.when(j > c)
             def _():
@@ -231,30 +258,38 @@
         bias[...] = jnp.where(
             lax.broadcasted_iota(jnp.int32, (tokens, keys), 1)
             <= c * tokens + lax.broadcasted_iota(jnp.int32, (tokens, keys), 0), 0.0, -1e30)
-        for d in range(1, ranks):
-            @pl.when(c >= d)
-            def _():
-                where = {"ctx": c}
-                remote(k_ref.at[0], kbuf.at[c - d], kv_send.at[d, 0], kv_recv.at[c - d, 0], where).wait_recv()
-                remote(v_ref.at[0], vbuf.at[c - d], kv_send.at[d, 1], kv_recv.at[c - d, 1], where).wait_recv()
-
-        def attend(step, _):
-            for r in range(together):
-                h = step * together + r
-                at = pl.ds(pl.multiple_of(h * HEAD_DIM, HEAD_DIM), HEAD_DIM)
-                g = (step * together) // group
-                kv_at = pl.ds(pl.multiple_of(g * HEAD_DIM, HEAD_DIM), HEAD_DIM)
-                kk = kbuf[:, :, kv_at].reshape(keys, HEAD_DIM)
-                vv = vbuf[:, :, kv_at].reshape(keys, HEAD_DIM)
-                s = lax.dot_general(q_ref[0, :, at], kk, (((1,), (1,)), ((), ())),
+        q_copy.wait()
+
+        def attend(i):
+            g = i // (chunks // kv_heads)
+
+            @pl.when(lax.rem(i, chunks // kv_heads) == 0)
+            def _():
+                for d in range(1, ranks):
+                    @pl.when(c >= d)
+                    def _():
+                        wait_kv(d, g)
+            kk = kbuf[:, g].reshape(keys, HEAD_DIM)
+            vv = vbuf[:, g].reshape(keys, HEAD_DIM)
+            for r in range(chunk // HEAD_DIM):
+                at = pl.ds(pl.multiple_of(i * chunk + r * HEAD_DIM, HEAD_DIM), HEAD_DIM)
+                s = lax.dot_general(q_ref[:, at], kk, (((1,), (1,)), ((), ())),
                                     preferred_element_type=F32)
                 s = s * (LOG2E * HEAD_DIM ** -0.5) + bias[...]
                 terms = jnp.exp2(s - jnp.max(s, axis=1, keepdims=True))
                 weighted = dot32(terms.astype(BF16), vv)
                 att[:, at] = weighted * (1.0 / jnp.sum(terms, axis=1, keepdims=True))
+
+        def main(i, _):
+            finish_mix(i, 0)
+            attend(i)
             return 0
 
-        lax.fori_loop(0, q_heads // together, attend, 0)
+        lax.fori_loop(0, chunks, main, 0)
+
+        @pl.when(p == 0)
+        def _():
+            in_copy.wait()
 
         sq_mine[...] = jnp.zeros_like(sq_mine)
 
@@ -299,8 +334,9 @@
             @pl.when(c + d < ranks)
             def _():
                 tot_copy(d).wait_send()
-                for copy in kv_copies(d):
-                    copy.wait_send()
+                for g in range(kv_heads):
+                    for copy in kv_copies(d, g):
+                        copy.wait_send()
         for level in range(levels):
             @pl.when(sends_at(level))
             def _():
@@ -318,8 +354,18 @@
             lax.fori_loop(0, chunks, drain, 0)
 
     scratch = [
-        pltpu.VMEM((ranks, tokens, kv_width), BF16),
-        pltpu.VMEM((ranks, tokens, kv_width), BF16),
+        pltpu.VMEM((tokens, width), BF16),
+        pltpu.VMEM((nstate, tokens), BF16),
+        pltpu.VMEM((nstate, tokens), BF16),
+        pltpu.VMEM((heads, tokens), F32),
+        pltpu.VMEM((1, heads), F32),
+        pltpu.VMEM((tokens, width), BF16),
+        pltpu.VMEM((1, width), F32),
+        pltpu.SemaphoreType.DMA((7,)),
+        pltpu.SemaphoreType.DMA((chunks,)),
+        pltpu.SemaphoreType.DMA((kv_heads, 2)),
+        pltpu.VMEM((ranks, kv_heads, tokens, HEAD_DIM), BF16),
+        pltpu.VMEM((ranks, kv_heads, tokens, HEAD_DIM), BF16),
         pltpu.VMEM((tokens, keys), F32),
         pltpu.VMEM((tokens, width), BF16),
         pltpu.VMEM((tokens, width), F32),
@@ -339,8 +385,8 @@
         pltpu.VMEM((max(exps - 1, 1), tokens, 128), F32),
         pltpu.SemaphoreType.DMA((ranks // 2, chunks)),
         pltpu.SemaphoreType.DMA((levels, chunks)),
-        pltpu.SemaphoreType.DMA((ranks, 2)),
-        pltpu.SemaphoreType.DMA((ranks, 2)),
+        pltpu.SemaphoreType.DMA((ranks, kv_heads, 2)),
+        pltpu.SemaphoreType.DMA((ranks, kv_heads, 2)),
         pltpu.SemaphoreType.DMA((ranks,)),
         pltpu.SemaphoreType.DMA((ranks,)),
         pltpu.SemaphoreType.DMA((chunks,)),
@@ -367,12 +413,13 @@
         return pl.pallas_call(
             kernel,
             out_shape=(shape, shape),
-            in_specs=[vmem] * 10,
+            in_specs=[pl.BlockSpec(memory_space=pltpu.HBM)] * 10,
             out_specs=(vmem, vmem),
             scratch_shapes=scratch,
             compiler_params=pltpu.CompilerParams(
-                collective_id=0, has_side_effects=True, vmem_limit_bytes=48 * 2 ** 20),
-        )(mix_input, state_write, state_read, log_decay, skip_gain[None], query_rows, key_rows,
+                collective_id=0, has_side_effects=True, vmem_limit_bytes=60 * 2 ** 20),
+        )(mix_input, jnp.swapaxes(state_write, 1, 2), jnp.swapaxes(state_read, 1, 2),
+          jnp.swapaxes(log_decay, 1, 2), skip_gain[None], query_rows, key_rows,
           value_rows, incoming, norm_gain[None])
 
     placed = (

time: 52.9 us -> 46.7 us (0.88)
  the two profiles are of different devices: /device:TPU:7 before, /device:TPU:15 now
where the time goes in v2:
time: 46.7 us; the launch traced here: 46.5 us
  Pallas kernels  42.5 us (91%)
  local copies, waits for them, and re-layouts  3.35 us (7%)
  between operations  0.65 us (1%)
    pallas_call x1, Pallas kernels, body(): pl.pallas_call(kernel, out_shape=(shape, shape), in_specs=[pl.BlockSpec(m...  42.5 us
    unnamed x4, local copies, waits for them, and re-layouts  3.35 us

profile of v2, /device:TPU:15, one launch (start us, length us, event | category | flops | bytes accessed | tf_op | source)
XLA Modules:
  0.0 46.5 jit_solution(10035658353414485399)
XLA Ops:
  0.6 42.5 %shard_map.113 = (bf16[1,128,4096]{2,1,0:T(8,128)(2,1)}, bf16[1,128,4096]{2,1,0:T(8,128)(2,1)}) custom-call(bf16[1,128,4096]{2,1,0:T(8,128)(2,1)} %x_hbm.1, bf16[1,64,128]{2,1,0:T(8,128)(2,1)} %bitcast.6, bf16[1,64,128]{2,1,0:T(8,128)(2,1)} %bitcast.7, f32[1,64,128]{2,1,0:T(8,128)} %bitcast.5, f32[1,64]{1,0:T(1,128)} %bitcast.9, ...), custom_call_target="tpu_custom_call" | custom-call | tf_op jit(solution)/shard_map/pallas_call | solution.py:413
  43.1 0.0 copy-start
  43.2 2.4 %copy.14 = bf16[1,128,4096]{2,1,0:T(8,128)(2,1)} copy(bf16[1,128,4096]{2,1,0:T(8,128)(2,1)} %get-tuple-element.4) | data formatting | bytes 2097152
  45.5 0.0 copy-done
  45.5 1.0 %copy.15 = bf16[1,128,4096]{2,1,0:T(8,128)(2,1)} copy(bf16[1,128,4096]{2,1,0:T(8,128)(2,1)S(1)} %copy-done) | data formatting | bytes 2097152
Async XLA Ops:
  43.1 2.4 %copy-start = (bf16[1,128,4096]{2,1,0:T(8,128)(2,1)S(1)}, bf16[1,128,4096]{2,1,0:T(8,128)(2,1)}, u32[]{:S(2)}) copy-start(bf16[1,128,4096]{2,1,0:T(8,128)(2,1)} %get-tuple-element.5) | copy-start | bytes 3145732

commit v3 on v2

--- a/solution.py
+++ b/solution.py
@@ -145,50 +145,15 @@
             remote(kbuf.at[j, g], kbuf.at[j, g], kv_send.at[d, g, 0], kv_recv.at[j, g, 0], where).wait_recv()
             remote(vbuf.at[j, g], vbuf.at[j, g], kv_send.at[d, g, 1], kv_recv.at[j, g, 1], where).wait_recv()
 
-        def make_local(i, _):
-            at = pl.ds(pl.multiple_of(i * chunk, chunk), chunk)
-            own_x(i).wait()
-            mat = spread_mat[:, at]
-            scaled = (dot32(tail[0], mat) + dot32(tail[1], mat)) * x_ref[:, at].astype(F32)
-            state = dot32(write_ref[...], scaled.astype(BF16))
-            local[:, at] = state
-
-            @pl.when(lax.rem(c, 2) == 0)
-            def _():
-                outbox[:, at] = state.astype(BF16)
-                state_copy(0, 0, i).start()
-
-            @pl.when(lax.rem(i, chunks // kv_heads) == 0)
-            def _():
-                g = i // (chunks // kv_heads)
-                for copy in own_kv(g):
-                    copy.wait()
-                for d in range(1, ranks):
-                    @pl.when(c + d < ranks)
-                    def _():
-                        for copy in kv_copies(d, g):
-                            copy.start()
-            return 0
-
-        lax.fori_loop(0, chunks, make_local, 0)
-
-        for d in range(1, ranks):
-            @pl.when(c >= d)
-            def _():
-                remote(tot_mine, tot_all.at[c - d], tt_send.at[d], tt_recv.at[c - d],
-                       {"ctx": c}).wait_recv()
-        def expand_row(logs):
-            parts = split_two(jnp.exp2(logs)[:, :heads])
-            return dot32(parts[0], spread_mat[...]) + dot32(parts[1], spread_mat[...])
-
-        dtot[0] = expand_row(tot_mine[...])
         dtot[1] = dot32(skips[0], spread_mat[...]) + dot32(skips[1], spread_mat[...])
-        for level in range(1, levels):
-            base = (c // 2 ** level) * 2 ** level
-            logs = jnp.zeros((8, 128), F32)
-            for j in range(ranks):
-                logs = logs + jnp.where((j >= base) & (j < c), tot_all[j], 0.0)
-            dvec[level] = expand_row(logs)
+        def send_kv(g):
+            for copy in own_kv(g):
+                copy.wait()
+            for d in range(1, ranks):
+                @pl.when(c + d < ranks)
+                def _():
+                    for copy in kv_copies(d, g):
+                        copy.start()
 
         def receive(i):
             at = pl.ds(pl.multiple_of(i * chunk, chunk), chunk)
@@ -224,6 +189,10 @@
                     def _():
                         for d in range(2 ** level):
                             state_copy(level, d, i).start()
+
+            @pl.when((lax.rem(c, 2) == 1) & (lax.rem(i, chunks // kv_heads) == 0))
+            def _():
+                send_kv(i // (chunks // kv_heads))
 
             mat = spread_mat[:, at]
             grown = dot32(since[0], mat) + dot32(since[1], mat)
@@ -250,6 +219,47 @@
                 onward(i).start()
             return 0
 
+        def make_local(i, _):
+            at = pl.ds(pl.multiple_of(i * chunk, chunk), chunk)
+            own_x(i).wait()
+            mat = spread_mat[:, at]
+            scaled = (dot32(tail[0], mat) + dot32(tail[1], mat)) * x_ref[:, at].astype(F32)
+            state = dot32(write_ref[...], scaled.astype(BF16))
+            local[:, at] = state
+
+            @pl.when(lax.rem(c, 2) == 0)
+            def _():
+                outbox[:, at] = state.astype(BF16)
+                state_copy(0, 0, i).start()
+
+            @pl.when((lax.rem(c, 2) == 0) & (lax.rem(i, chunks // kv_heads) == 0))
+            def _():
+                send_kv(i // (chunks // kv_heads))
+
+            @pl.when(c == 0)
+            def _():
+                finish_mix(i, 0)
+            return 0
+
+        lax.fori_loop(0, chunks, make_local, 0)
+
+        for d in range(1, ranks):
+            @pl.when(c >= d)
+            def _():
+                remote(tot_mine, tot_all.at[c - d], tt_send.at[d], tt_recv.at[c - d],
+                       {"ctx": c}).wait_recv()
+        def expand_row(logs):
+            parts = split_two(jnp.exp2(logs)[:, :heads])
+            return dot32(parts[0], spread_mat[...]) + dot32(parts[1], spread_mat[...])
+
+        dtot[0] = expand_row(tot_mine[...])
+        for level in range(1, levels):
+            base = (c // 2 ** level) * 2 ** level
+            logs = jnp.zeros((8, 128), F32)
+            for j in range(ranks):
+                logs = logs + jnp.where((j >= base) & (j < c), tot_all[j], 0.0)
+            dvec[level] = expand_row(logs)
+
         for j in range(1, ranks):
             @pl.when(j > c)
             def _():
@@ -280,12 +290,28 @@
                 weighted = dot32(terms.astype(BF16), vv)
                 att[:, at] = weighted * (1.0 / jnp.sum(terms, axis=1, keepdims=True))
 
-        def main(i, _):
-            finish_mix(i, 0)
+        def attend_one(i, _):
             attend(i)
             return 0
 
-        lax.fori_loop(0, chunks, main, 0)
+        lag = 1
+
+        @pl.when(c > 0)
+        def _():
+            def main(i, _):
+                @pl.when(i < chunks)
+                def _():
+                    finish_mix(i, 0)
+
+                @pl.when(i >= lag)
+                def _():
+                    attend(i - lag)
+                return 0
+            lax.fori_loop(0, chunks + lag, main, 0)
+
+        @pl.when(c == 0)
+        def _():
+            lax.fori_loop(0, chunks, attend_one, 0)
 
         @pl.when(p == 0)
         def _():

time: 46.7 us -> 44.3 us (0.949)
  Pallas kernels: 42.5 us -> 40.1 us
    pallas_call x1, Pallas kernels: 42.5 us -> 40.1 us  [body(): pl.pallas_call(kernel, out_shape=(shape, shape), in_specs=[pl.BlockSpec(m...]
where the time goes in v3:
time: 44.3 us; the launch traced here: 44.1 us
  Pallas kernels  40.1 us (91%)
  local copies, waits for them, and re-layouts  3.35 us (8%)
  between operations  0.65 us (1%)
    pallas_call x1, Pallas kernels, body(): pl.pallas_call(kernel, out_shape=(shape, shape), in_specs=[pl.BlockSpec(m...  40.1 us
    unnamed x4, local copies, waits for them, and re-layouts  3.35 us

profile of v3, /device:TPU:15, one launch (start us, length us, event | category | flops | bytes accessed | tf_op | source)
XLA Modules:
  0.0 44.1 jit_solution(348879247693109960)
XLA Ops:
  0.6 40.1 %shard_map.113 = (bf16[1,128,4096]{2,1,0:T(8,128)(2,1)}, bf16[1,128,4096]{2,1,0:T(8,128)(2,1)}) custom-call(bf16[1,128,4096]{2,1,0:T(8,128)(2,1)} %x_hbm.1, bf16[1,64,128]{2,1,0:T(8,128)(2,1)} %bitcast.6, bf16[1,64,128]{2,1,0:T(8,128)(2,1)} %bitcast.7, f32[1,64,128]{2,1,0:T(8,128)} %bitcast.5, f32[1,64]{1,0:T(1,128)} %bitcast.9, ...), custom_call_target="tpu_custom_call" | custom-call | tf_op jit(solution)/shard_map/pallas_call | solution.py:439
  40.8 0.0 copy-start
  40.8 2.4 %copy.14 = bf16[1,128,4096]{2,1,0:T(8,128)(2,1)} copy(bf16[1,128,4096]{2,1,0:T(8,128)(2,1)} %get-tuple-element.4) | data formatting | bytes 2097152
  43.1 0.0 copy-done
  43.1 1.0 %copy.15 = bf16[1,128,4096]{2,1,0:T(8,128)(2,1)} copy(bf16[1,128,4096]{2,1,0:T(8,128)(2,1)S(1)} %copy-done) | data formatting | bytes 2097152
Async XLA Ops:
  40.8 2.4 %copy-start = (bf16[1,128,4096]{2,1,0:T(8,128)(2,1)S(1)}, bf16[1,128,4096]{2,1,0:T(8,128)(2,1)}, u32[]{:S(2)}) copy-start(bf16[1,128,4096]{2,1,0:T(8,128)(2,1)} %get-tuple-element.5) | copy-start | bytes 3145732
